TPU v7x, 512 devices: a whole 4x8x8 slice. The times are simulated.
512 devices in a mesh: seq: 32 (over x, y), req: 16 (over z, core).
Axes of the slice: x: 4, y: 8, z: 8, core: 2. Of those that a mesh axis runs over, the one named last changes fastest.
Arguments:
- x_in: bfloat16 [96, 4, 1536], P('req'), may hold values from -6 to 6
- attn_gain: float32 [1536], replicated, may hold values from 0.25 to 1.75
- moe_gain: float32 [1536], replicated, may hold values from 0.25 to 1.75
- w_qkv: bfloat16 [1536, 2560], P(None, 'seq'), may hold values from -0.15625 to 0.15625
- w_o: bfloat16 [1536, 1536], P(None, 'seq'), may hold values from -0.3125 to 0.3125
- cache_k: bfloat16 [96, 4096, 512], P('req', 'seq'), may hold values from -1024 to 1024
- cache_v: bfloat16 [96, 4096, 512], P('req', 'seq'), may hold values from -6 to 6
- page_map: int32 [96, 256], P('req', 'seq'), may hold values from 0 to 255, as said below
- lengths: int32 [96], P('req'), may hold values from 2 to 4096, as said below
- routes: int32 [96, 4, 8], P('req'), may hold values from 0 to 31, all different within a row; in each aligned block of 24 rows (0 to 23, 24 to 47, ..., all dimensions but the last counted through in order) at most 12 rows name the same one
- route_weights: float32 [96, 4, 8], P('req'), may hold values from 0.1 to 1
- w_gate_up: bfloat16 [32, 1536, 1024], P('seq', 'req'), may hold values from -0.15625 to 0.15625
- w_down: bfloat16 [32, 512, 1536], P('seq', None, 'req'), may hold values from -0.375 to 0.375
Outputs:
- layer_out: bfloat16 [96, 4, 1536], P('req', None, 'seq')
Inputs may be any that keep to these rules, and one draw needn't show every extreme that they name: `lengths`: every index of req holds one request with exactly 4096 cached positions. `page_map`: each row is a permutation of the request's 256 logical pages. `routes`: A token names 8 different experts. Among the 24 tokens of one index of req no expert is named more than 12 times.
All inputs are finite; a program needn't handle non-finite values.
Results may differ from a plain program's by a relative error of at most 0.01.
Values may be sent and summed in bfloat16 or wider, within the bound.
A program may use at most 64 MiB of HBM per device.

v0:
```python
import math
import jax
import jax.numpy as jnp
from jax import lax
from jax.sharding import PartitionSpec as P

D = 1536
HEADS = 24
KVH = 8
HD = 64
FFE = 512
TOP = 8
NSTEP = 4
PAGE = 16
ATT = 1536
KVD = 512
GROUP = 3
CAP = 12
EPS = 1e-05
NEG = -1e30


def normalize(values, gain):
    power = jnp.mean(values * values, axis=-1, keepdims=True)
    return values * lax.rsqrt(power + EPS) * gain


def rotate(values, position):
    half = values.shape[-1] // 2
    rates = jnp.exp(
        jnp.arange(half, dtype=jnp.float32) * (-2.0 * math.log(10000.0) / values.shape[-1])
    )
    angle = position[..., None, None] * rates
    cosine = jnp.cos(angle)
    sine = jnp.sin(angle)
    first_half = values[..., :half]
    second_half = values[..., half:]
    return jnp.concatenate(
        [first_half * cosine - second_half * sine, second_half * cosine + first_half * sine],
        axis=-1,
    )


def gather_columns(part, axis_name):
    count = lax.axis_size(axis_name)
    copies = jnp.broadcast_to(part[None], (count,) + part.shape)
    pieces = lax.all_to_all(copies, axis_name, split_axis=0, concat_axis=0, tiled=True)
    rows, width = part.shape
    return jnp.moveaxis(pieces, 0, 1).reshape(rows, count * width)


def sum_scatter_columns(value, axis_name):
    count = lax.axis_size(axis_name)
    rows, width = value.shape
    chunks = jnp.moveaxis(value.reshape(rows, count, width // count), 1, 0)
    pieces = lax.all_to_all(chunks, axis_name, split_axis=0, concat_axis=0, tiled=True)
    return jnp.sum(pieces, axis=0)


def local(
    x_in,
    attn_gain,
    moe_gain,
    w_qkv,
    w_o,
    cache_k,
    cache_v,
    page_map,
    lengths,
    routes,
    route_weights,
    w_gate_up,
    w_down,
):
    pieces = 4
    expert_in = jnp.concatenate(
        [
            lax.all_gather(part, "req", axis=0, tiled=True)
            for part in jnp.split(w_gate_up[0], pieces, axis=1)
        ],
        axis=1,
    )
    expert_out = jnp.concatenate(
        [
            lax.all_gather(part, "req", axis=1, tiled=True)
            for part in jnp.split(w_down[0], pieces // 2, axis=0)
        ],
        axis=0,
    )
    seq_count = lax.axis_size("seq")
    me = lax.axis_index("seq")
    local_requests = x_in.shape[0]
    row_count = local_requests * NSTEP
    inputs = x_in.astype(jnp.float32).reshape(row_count, D)
    normed = normalize(inputs, attn_gain).astype(jnp.bfloat16)
    projected = gather_columns(jnp.dot(normed, w_qkv, preferred_element_type=jnp.float32), "seq")
    queries = projected[:, :ATT].reshape(local_requests, NSTEP, HEADS, HD)
    keys_new = projected[:, ATT : ATT + KVD].reshape(local_requests, NSTEP, KVH, HD)
    values_new = (
        projected[:, ATT + KVD :].reshape(local_requests, NSTEP, KVH, HD).astype(jnp.bfloat16)
    )
    position = (lengths[:, None] + jnp.arange(NSTEP, dtype=jnp.int32)[None, :]).astype(jnp.float32)
    queries = (
        rotate(queries, position)
        .astype(jnp.bfloat16)
        .reshape(local_requests, NSTEP, KVH, GROUP, HD)
    )
    keys_new = rotate(keys_new, position).astype(jnp.bfloat16)
    scale = HD ** (-0.5)
    slot_count = cache_k.shape[1]
    cached_keys = cache_k.reshape(local_requests, slot_count, KVH, HD)
    cached_values = cache_v.reshape(local_requests, slot_count, KVH, HD)
    slot_position = (
        page_map[:, :, None] * PAGE + jnp.arange(PAGE, dtype=jnp.int32)[None, None, :]
    ).reshape(local_requests, slot_count)
    live = (slot_position < lengths[:, None])[:, None, None, None, :]
    scores = (
        jnp.einsum("rskgd,rtkd->rskgt", queries, cached_keys, preferred_element_type=jnp.float32)
        * scale
    )
    scores = jnp.where(live, scores, NEG)
    local_top = jnp.max(scores, axis=-1)
    exp_scores = jnp.where(live, jnp.exp(scores - local_top[..., None]), 0.0)
    local_total = jnp.sum(exp_scores, axis=-1).reshape(row_count, HEADS)
    local_sums = jnp.einsum(
        "rskgt,rtkd->rskgd",
        exp_scores.astype(jnp.bfloat16),
        cached_values,
        preferred_element_type=jnp.float32,
    ).reshape(row_count, ATT)
    local_top = local_top.reshape(row_count, HEADS)
    width = ATT // seq_count
    sum_chunks = jnp.moveaxis(local_sums.reshape(row_count, seq_count, width), 1, 0)
    extras = jnp.broadcast_to(
        jnp.concatenate([local_total, local_top], axis=1)[None], (seq_count, row_count, 2 * HEADS)
    )
    outgoing = jnp.concatenate([sum_chunks, extras], axis=2)
    arrived = lax.all_to_all(outgoing, "seq", split_axis=0, concat_axis=0, tiled=True)
    part_sums = arrived[:, :, :width]
    part_totals = arrived[:, :, width : width + HEADS]
    part_tops = arrived[:, :, width + HEADS :]
    causal = (
        jnp.arange(NSTEP, dtype=jnp.int32)[:, None] >= jnp.arange(NSTEP, dtype=jnp.int32)[None, :]
    )[None, :, None, None, :]
    fresh = (
        jnp.einsum("rskgd,rukd->rskgu", queries, keys_new, preferred_element_type=jnp.float32)
        * scale
    )
    fresh = jnp.where(causal, fresh, NEG).reshape(row_count, HEADS, NSTEP)
    cache_top = jnp.max(part_tops, axis=0)
    highest = jnp.maximum(cache_top, jnp.max(fresh, axis=-1))
    factors = jnp.exp(part_tops - highest[None])
    fresh_exp = jnp.exp(fresh - highest[:, :, None])
    denominator = jnp.sum(part_totals * factors, axis=0) + jnp.sum(fresh_exp, axis=-1)
    fresh_probs = fresh_exp.reshape(local_requests, NSTEP, KVH, GROUP, NSTEP).astype(jnp.bfloat16)
    fresh_sums = jnp.einsum(
        "rskgu,rukd->rskgd", fresh_probs, values_new, preferred_element_type=jnp.float32
    ).reshape(row_count, ATT)
    start = me * width
    head_of = (start + jnp.arange(width, dtype=jnp.int32)) // HD
    chunk_factors = jnp.take(factors, head_of, axis=2)
    numerator = jnp.sum(part_sums * chunk_factors, axis=0) + lax.dynamic_slice_in_dim(
        fresh_sums, start, width, 1
    )
    chunk_denominator = jnp.take(denominator, head_of, axis=1)
    attended_part = (numerator / chunk_denominator).astype(jnp.bfloat16)
    attended = gather_columns(attended_part, "seq")
    attn_mixed = gather_columns(jnp.dot(attended, w_o, preferred_element_type=jnp.float32), "seq")
    resid = inputs + attn_mixed
    mixed_in = normalize(resid, moe_gain).astype(jnp.bfloat16)
    expert = me
    chosen = routes.reshape(row_count, TOP)
    gates = route_weights.reshape(row_count, TOP)
    route_scale = jnp.sum(jnp.where(chosen == expert, gates, 0.0), axis=-1)
    gate_up = jnp.dot(mixed_in, expert_in, preferred_element_type=jnp.float32)
    hidden = (jax.nn.silu(gate_up[:, :FFE]) * gate_up[:, FFE:]).astype(jnp.bfloat16)
    produced = jnp.dot(hidden, expert_out, preferred_element_type=jnp.float32)
    own_share = sum_scatter_columns(route_scale[:, None] * produced, "seq")
    share_width = own_share.shape[1]
    resid_share = lax.dynamic_slice_in_dim(resid, me * share_width, share_width, 1)
    return (
        (resid_share + own_share).astype(jnp.bfloat16).reshape(local_requests, NSTEP, share_width)
    )


def solution(mesh):
    in_specs = (
        P("req", None, None),
        P(),
        P(),
        P(None, "seq"),
        P(None, "seq"),
        P("req", "seq", None),
        P("req", "seq", None),
        P("req", "seq"),
        P("req"),
        P("req", None, None),
        P("req", None, None),
        P("seq", "req", None),
        P("seq", None, "req"),
    )
    out_specs = P("req", None, "seq")
    return jax.shard_map(local, mesh=mesh, in_specs=in_specs, out_specs=out_specs, check_vma=False)
```

profile of v0, /device:TPU:8, one launch (start us, length us, event | category | flops | bytes accessed | tf_op | source)
XLA Modules:
  0.0 217.1 jit_solution(889715388834273330)
XLA Ops:
  0.0 0.9 reshape.269
  0.9 1.0 multiply_reduce_fusion.2
  2.1 1.0 fusion.26
  3.1 0.8 broadcast_in_dim.66
  3.9 10.2 %all-to-all-start = ((f32[32,24,80]{2,1,0:T(8,128)}), f32[32,24,80]{2,1,0:T(8,128)S(1)}, u32[]{:S(2)}, u32[]{:S(2)}) async-start(f32[32,24,80]{2,1,0:T(8,128)} %broadcast_in_dim.66), calls=%async_computation | async-start | bytes 786432 | tf_op jit(solution)/shard_map/all_to_all | solution.py:47
  14.4 0.4 copy.66
  14.8 0.8 copy-done.4
  15.5 1.2 copy.67
  16.8 25.3 %all_gather.18 = bf16[1536,256]{1,0:T(8,128)(2,1)S(1)} all-gather(bf16[96,256]{1,0:T(8,128)(2,1)S(1)} %get-tuple-element.14), channel_id=1, replica_groups=mesh['seq'=32,'req'=16] {'req'}, dimensions={0}, use_global_device_ids=true | all-gather | bytes 835584 | tf_op jit(solution)/shard_map/all_gather | solution.py:78
  42.1 18.1 %all_gather.19 = bf16[1536,256]{1,0:T(8,128)(2,1)} all-gather(bf16[96,256]{1,0:T(8,128)(2,1)S(1)} %get-tuple-element.17), channel_id=1, replica_groups=mesh['seq'=32,'req'=16] {'req'}, dimensions={0}, use_global_device_ids=true | all-gather | bytes 835584 | tf_op jit(solution)/shard_map/all_gather | solution.py:78
  60.2 19.3 %all_gather.20 = bf16[1536,256]{1,0:T(8,128)(2,1)} all-gather(bf16[96,256]{1,0:T(8,128)(2,1)S(1)} %get-tuple-element.16), channel_id=1, replica_groups=mesh['seq'=32,'req'=16] {'req'}, dimensions={0}, use_global_device_ids=true | all-gather | bytes 835584 | tf_op jit(solution)/shard_map/all_gather | solution.py:78
  79.6 0.2 multiply_cosine_fusion
  79.8 18.0 %all_gather.21 = bf16[1536,256]{1,0:T(8,128)(2,1)} all-gather(bf16[96,256]{1,0:T(8,128)(2,1)S(1)} %get-tuple-element.15), channel_id=1, replica_groups=mesh['seq'=32,'req'=16] {'req'}, dimensions={0}, use_global_device_ids=true | all-gather | bytes 835584 | tf_op jit(solution)/shard_map/all_gather | solution.py:78
  97.9 0.2 reshape.270
  98.3 0.2 subtract_convert_fusion
  98.5 0.4 copy-done.1
  99.0 0.5 fusion.47
  99.5 0.4 copy.70
  99.9 0.5 fusion.18
  100.4 0.4 copy.69
  101.0 0.6 convolution_bitcast_fusion
  101.6 0.1 copy.68
  101.7 0.3 reshape_reshape.3
  102.0 0.2 copy.71
  102.4 0.9 pad_maximum_fusion
  103.3 9.9 %all-to-all-start.1 = ((f32[32,24,96]{2,1,0:T(8,128)}), f32[32,24,96]{2,1,0:T(8,128)S(1)}, u32[]{:S(2)}, u32[]{:S(2)}) async-start(f32[32,24,96]{2,1,0:T(8,128)} %pad_maximum_fusion), calls=%async_computation.1 | async-start | bytes 786432 | tf_op jit(solution)/shard_map/all_to_all | solution.py:138
  113.6 1.1 fusion.48
  114.9 13.8 %all-to-all-done.1 = f32[32,24,96]{2,1,0:T(8,128)S(1)} async-done(((f32[32,24,96]{2,1,0:T(8,128)}), f32[32,24,96]{2,1,0:T(8,128)S(1)}, u32[]{:S(2)}, u32[]{:S(2)}) %all-to-all-start.1) | async-done | bytes 294944 | tf_op jit(solution)/shard_map/all_to_all | solution.py:138
  128.6 0.3 slice_reduce_fusion
  129.1 0.3 fusion.16
  129.4 0.4 convolution_bitcast_fusion.1
  129.9 0.3 reshape.277
  130.3 0.2 copy.106
  130.5 0.2 copy.110
  130.7 0.3 copy.105
  131.1 0.3 multiply_reduce_fusion
  131.4 0.6 gather_fusion
  132.1 0.6 gather_fusion.1
  132.6 0.3 fusion.15
  133.2 0.9 reshape.308
  134.1 4.8 %all-to-all-start.2 = ((bf16[32,2,576]{2,1,0:T(2,128)(2,1)}), bf16[32,2,576]{2,1,0:T(2,128)(2,1)S(1)}, u32[]{:S(2)}, u32[]{:S(2)}) async-start(bf16[32,2,576]{2,1,0:T(2,128)(2,1)} %reshape.308), calls=%async_computation.2 | async-start | bytes 163840 | tf_op jit(solution)/shard_map/all_to_all | solution.py:47
  138.9 19.5 %all-gather = bf16[1,256,1536]{1,2,0:T(8,128)(2,1)} all-gather(bf16[1,256,96]{1,2,0:T(8,128)(2,1)S(1)} %get-tuple-element.20), channel_id=2, replica_groups=mesh['seq'=32,'req'=16] {'req'}, dimensions={2}, use_global_device_ids=true | all-gather | bytes 835584 | tf_op jit(solution)/shard_map/all_gather | solution.py:85
  158.5 0.2 reshape.309
  158.8 0.3 reshape.278
  159.1 0.1 fusion.49
  159.3 1.0 reshape.310
  160.3 9.8 %all-to-all-start.3 = ((f32[32,1,1152]{2,1,0:T(1,128)}), f32[32,1,1152]{2,1,0:T(1,128)S(1)}, u32[]{:S(2)}, u32[]{:S(2)}) async-start(f32[32,1,1152]{2,1,0:T(1,128)} %reshape.310), calls=%async_computation.3 | async-start | bytes 294912 | tf_op jit(solution)/shard_map/all_to_all | solution.py:47
  170.1 18.0 %all-gather.1 = bf16[1,256,1536]{1,2,0:T(8,128)(2,1)} all-gather(bf16[1,256,96]{1,2,0:T(8,128)(2,1)S(1)} %get-tuple-element.21), channel_id=3, replica_groups=mesh['seq'=32,'req'=16] {'req'}, dimensions={2}, use_global_device_ids=true | all-gather | bytes 835584 | tf_op jit(solution)/shard_map/all_gather | solution.py:85
  188.1 0.5 broadcast.243
  188.6 1.0 reduce.5
  189.6 0.2 reshape.311
  189.9 0.2 reshape.279
  190.1 0.3 reshape.280
  190.4 0.4 copy-done.9
  190.8 0.1 multiply_reduce_fusion.1
  191.1 2.6 %fusion = f32[24,1024]{1,0:T(8,128)S(1)} fusion(bf16[1536,256]{1,0:T(8,128)(2,1)} %all_gather.21, bf16[1536,256]{1,0:T(8,128)(2,1)} %all_gather.20, bf16[1536,256]{1,0:T(8,128)(2,1)S(1)} %copy-done.5, bf16[1536,256]{1,0:T(8,128)(2,1)S(1)} %all_gather.18, f32[24,1536]{1,0:T(8,128)S(1)} %add.165, f32[1536]{0:T(1024)S(1)} %copy-done.17, f32[24]{0:T(128)S(1)} %rsqrt.25), kind=kOutput, calls=%fused_computation.2 | convolution fusion | flops 88190976 | bytes 3397728 | tf_op jit(solution)/shard_map/dot_general | solution.py:175
  193.7 0.5 convolution_multiply_fusion
  194.2 0.2 reshape.281
  194.4 0.2 copy.120
  194.6 0.4 reshape.312
  195.0 20.2 %all_to_all.25 = f32[32,1,1152]{2,1,0:T(1,128)S(1)} all-to-all(f32[32,1,1152]{2,1,0:T(1,128)S(1)} %reshape.312), channel_id=1, replica_groups=mesh['seq'=32,'req'=16] {'seq'}, dimensions={0} | all-to-all | bytes 294912 | tf_op jit(solution)/shard_map/all_to_all | solution.py:56
  215.2 1.0 reduce.6
  216.2 0.2 reshape.313
  216.4 0.7 add_convert_fusion.2
  (92 shorter events, 3.0 us)
Async XLA Ops:
  0.0 2.0 copy-start
  2.0 12.0 %copy-start.16 = (s32[6]{0:T(128)S(1)}, s32[6]{0:T(128)}, u32[]{:S(2)}) copy-start(s32[6]{0:T(128)} %param.21) | copy-start | bytes 76
  2.0 12.1 %copy-start.15 = (s32[6,8]{1,0:T(8,128)S(1)}, s32[6,8]{1,0:T(8,128)}, u32[]{:S(2)}) copy-start(s32[6,8]{1,0:T(8,128)} %param.20) | copy-start | bytes 580
  2.1 12.3 %copy-start.3 = (bf16[6,128,512]{2,1,0:T(8,128)(2,1)S(1)}, bf16[6,128,512]{2,1,0:T(8,128)(2,1)}, u32[]{:S(2)}) copy-start(bf16[6,128,512]{2,1,0:T(8,128)(2,1)} %param.18) | copy-start | bytes 2359300
  3.9 94.0 %all-to-all-start = ((f32[32,24,80]{2,1,0:T(8,128)}), f32[32,24,80]{2,1,0:T(8,128)S(1)}, u32[]{:S(2)}, u32[]{:S(2)}) async-start(f32[32,24,80]{2,1,0:T(8,128)} %broadcast_in_dim.66), calls=%async_computation | async-start | bytes 786432 | tf_op jit(solution)/shard_map/all_to_all | solution.py:47
  14.4 1.1 copy-start.4
  15.5 1.2 copy-start.10
  42.1 37.5 %copy-start.12 = (bf16[1,512,96]{1,2,0:T(8,128)(2,1)S(1)}, bf16[1,512,96]{1,2,0:T(8,128)(2,1)}, u32[]{:S(2)}) copy-start(bf16[1,512,96]{1,2,0:T(8,128)(2,1)} %param.25) | copy-start | bytes 294916
  98.2 0.7 copy-start.1
  99.5 1.5 copy-start.6
  102.4 10.9 %slice-start = ((f32[24,2560]{1,0:T(8,128)}), f32[24,512]{1,0:T(8,128)S(1)}, s32[]{:S(2)}) async-start(f32[24,2560]{1,0:T(8,128)} %copy-done.1), calls=%async_computation.5 | async-start | bytes 98304 | tf_op jit(solution)/shard_map/slice | solution.py:98
  103.3 10.1 %copy-start.2 = (f32[24,2560]{1,0:T(8,128)S(1)}, f32[24,2560]{1,0:T(8,128)}, u32[]{:S(2)}) copy-start(f32[24,2560]{1,0:T(8,128)} %copy-done.1) | copy-start | bytes 737284
  103.3 25.4 %all-to-all-start.1 = ((f32[32,24,96]{2,1,0:T(8,128)}), f32[32,24,96]{2,1,0:T(8,128)S(1)}, u32[]{:S(2)}, u32[]{:S(2)}) async-start(f32[32,24,96]{2,1,0:T(8,128)} %pad_maximum_fusion), calls=%async_computation.1 | async-start | bytes 786432 | tf_op jit(solution)/shard_map/all_to_all | solution.py:138
  132.9 25.4 %copy-start.13 = (f32[6,4,8]{2,1,0:T(4,128)S(1)}, f32[6,4,8]{2,1,0:T(4,128)}, u32[]{:S(2)}) copy-start(f32[6,4,8]{2,1,0:T(4,128)} %param.23) | copy-start | bytes 2308
  133.0 25.4 %copy-start.14 = (s32[6,4,8]{2,1,0:T(4,128)S(1)}, s32[6,4,8]{2,1,0:T(4,128)}, u32[]{:S(2)}) copy-start(s32[6,4,8]{2,1,0:T(4,128)} %param.22) | copy-start | bytes 2308
  134.1 24.4 %all-to-all-start.2 = ((bf16[32,2,576]{2,1,0:T(2,128)(2,1)}), bf16[32,2,576]{2,1,0:T(2,128)(2,1)S(1)}, u32[]{:S(2)}, u32[]{:S(2)}) async-start(bf16[32,2,576]{2,1,0:T(2,128)(2,1)} %reshape.308), calls=%async_computation.2 | async-start | bytes 163840 | tf_op jit(solution)/shard_map/all_to_all | solution.py:47
  138.9 20.2 %copy-start.11 = (bf16[1536,48]{0,1:T(8,128)(2,1)S(1)}, bf16[1536,48]{0,1:T(8,128)(2,1)}, u32[]{:S(2)}) copy-start(bf16[1536,48]{0,1:T(8,128)(2,1)} %param.17) | copy-start | bytes 442372
  160.3 27.8 %all-to-all-start.3 = ((f32[32,1,1152]{2,1,0:T(1,128)}), f32[32,1,1152]{2,1,0:T(1,128)S(1)}, u32[]{:S(2)}, u32[]{:S(2)}) async-start(f32[32,1,1152]{2,1,0:T(1,128)} %reshape.310), calls=%async_computation.3 | async-start | bytes 294912 | tf_op jit(solution)/shard_map/all_to_all | solution.py:47
  189.9 0.9 copy-start.9
  189.9 1.2 copy-start.5
  189.9 1.2 copy-start.17
  191.1 2.6 %copy-start.7 = (bf16[1,256,1536]{1,2,0:T(8,128)(2,1)S(1)}, bf16[1,256,1536]{1,2,0:T(8,128)(2,1)}, u32[]{:S(2)}) copy-start(bf16[1,256,1536]{1,2,0:T(8,128)(2,1)} %all-gather) | copy-start | bytes 2359300
  191.1 2.6 %copy-start.8 = (bf16[1,256,1536]{1,2,0:T(8,128)(2,1)S(1)}, bf16[1,256,1536]{1,2,0:T(8,128)(2,1)}, u32[]{:S(2)}) copy-start(bf16[1,256,1536]{1,2,0:T(8,128)(2,1)} %all-gather.1) | copy-start | bytes 2359300
where the time goes:
time: 218 us; the launch traced here: 217 us
  blocking collectives  139 us (64%)
  starting transfers between devices  34.6 us (16%)
  local copies, waits for them, and re-layouts  15.5 us (7%)
  waiting for transfers between devices  13.8 us (6%)
  other arithmetic  7.28 us (3%)
  matrix products  6.84 us (3%)
    all_gather x4, blocking collectives, local(): lax.all_gather(part, 'req', axis=0, tiled=True)  80.8 us
    all_gather x2, blocking collectives, local(): lax.all_gather(part, 'req', axis=1, tiled=True)  37.5 us
    all_to_all x3, starting transfers between devices, gather_columns(): lax.all_to_all(copies, axis_name, split_axis=0, concat_axis=0, tiled=True)  24.7 us
    all_to_all x1, blocking collectives, sum_scatter_columns(): lax.all_to_all(chunks, axis_name, split_axis=0, concat_axis=0, tiled=True)  20.2 us
    all_to_all x1, waiting for transfers between devices, local(): lax.all_to_all(outgoing, 'seq', split_axis=0, concat_axis=0, tiled=True)  13.8 us
    all_to_all x1, starting transfers between devices, local(): lax.all_to_all(outgoing, 'seq', split_axis=0, concat_axis=0, tiled=True)  9.92 us
    unnamed x49, local copies, waits for them, and re-layouts  6.93 us
  transfers between devices with their start and end apart: 4, of which 1 were waited for; matrix products, arithmetic and copies ran while one was open for 2% of the time, Pallas kernels for 0%

commit v1 on v0

--- a/solution.py
+++ b/solution.py
@@ -75,7 +75,9 @@
     pieces = 4
     expert_in = jnp.concatenate(
         [
-            lax.all_gather(part, "req", axis=0, tiled=True)
+            jnp.concatenate(
+                lax.all_to_all(jnp.stack([part] * lax.axis_size("req")), "req", 0, 0), axis=0
+            )
             for part in jnp.split(w_gate_up[0], pieces, axis=1)
         ],
         axis=1,

time: 218 us -> 257 us (1.18)
  waiting for transfers between devices: 13.8 us -> 53.3 us
  starting transfers between devices: 34.6 us -> 28 us
    all_gather x4 -> x0, blocking collectives: 80.8 us -> none  [local(): lax.all_gather(part, 'req', axis=0, tiled=True)]
    all_to_all x0 -> x3, blocking collectives: none -> 73.1 us  [the longest x2 58.3 us: local(): lax.all_to_all(jnp.stack([part] * lax.axis_size('req')), 'req', 0, 0)]
    all_to_all x3 -> x2, waiting for transfers between devices: 0.01 us -> 21.1 us  [gather_columns(): lax.all_to_all(copies, axis_name, split_axis=0, concat_axis=0, tiled=True)]
    all_to_all x0 -> x2, waiting for transfers between devices: none -> 19.4 us  [local(): lax.all_to_all(jnp.stack([part] * lax.axis_size('req')), 'req', 0, 0)]
    all_gather x2, blocking collectives: 37.5 us -> 53.2 us  [local(): lax.all_gather(part, 'req', axis=1, tiled=True)]
    all_to_all x3 -> x2, starting transfers between devices: 24.7 us -> 14.8 us  [gather_columns(): lax.all_to_all(copies, axis_name, split_axis=0, concat_axis=0, tiled=True)]
    all_to_all x0 -> x2, starting transfers between devices: none -> 8.24 us  [local(): lax.all_to_all(jnp.stack([part] * lax.axis_size('req')), 'req', 0, 0)]
    all_to_all x1, blocking collectives: 20.2 us -> 14.8 us  [sum_scatter_columns(): lax.all_to_all(chunks, axis_name, split_axis=0, concat_axis=0, tiled=True)]
  transfers between devices with their start and end apart: 4 -> 5, of which waited for: 1 -> 4; matrix products, arithmetic and copies ran while one was open for 2% -> 3% of each run, Pallas kernels for 0% -> 0%
where the time goes in v1:
time: 257 us; the launch traced here: 256 us
  blocking collectives  141 us (55%)
  waiting for transfers between devices  53.3 us (21%)
  starting transfers between devices  28 us (11%)
  local copies, waits for them, and re-layouts  16.9 us (7%)
  other arithmetic  8.68 us (3%)
  matrix products  7.42 us (3%)
    all_to_all x2, blocking collectives, local(): lax.all_to_all(jnp.stack([part] * lax.axis_size('req')), 'req', 0, 0)  58.3 us
    all_gather x2, blocking collectives, local(): lax.all_gather(part, 'req', axis=1, tiled=True)  53.2 us
    all_to_all x2, waiting for transfers between devices, gather_columns(): lax.all_to_all(copies, axis_name, split_axis=0, concat_axis=0, tiled=True)  21.1 us
    all_to_all x2, waiting for transfers between devices, local(): lax.all_to_all(jnp.stack([part] * lax.axis_size('req')), 'req', 0, 0)  19.4 us
    all_to_all x1, blocking collectives, gather_columns(): lax.all_to_all(copies, axis_name, split_axis=0, concat_axis=0, tiled=True)  14.9 us
    all_to_all x2, starting transfers between devices, gather_columns(): lax.all_to_all(copies, axis_name, split_axis=0, concat_axis=0, tiled=True)  14.8 us
    all_to_all x1, blocking collectives, sum_scatter_columns(): lax.all_to_all(chunks, axis_name, split_axis=0, concat_axis=0, tiled=True)  14.8 us
    all_to_all x1, waiting for transfers between devices, local(): lax.all_to_all(outgoing, 'seq', split_axis=0, concat_axis=0, tiled=True)  12.8 us
  transfers between devices with their start and end apart: 5, of which 4 were waited for; matrix products, arithmetic and copies ran while one was open for 3% of the time, Pallas kernels for 0%

profile of v1, /device:TPU:8, one launch (start us, length us, event | category | flops | bytes accessed | tf_op | source)
XLA Modules:
  0.0 256.0 jit_solution(8086912626894675753)
XLA Ops:
  0.0 0.9 reshape.289
  0.9 1.0 multiply_reduce_fusion.2
  2.1 1.0 fusion.26
  3.1 0.8 broadcast_in_dim.66
  3.9 10.2 %all-to-all-start = ((f32[32,24,80]{2,1,0:T(8,128)}), f32[32,24,80]{2,1,0:T(8,128)S(1)}, u32[]{:S(2)}, u32[]{:S(2)}) async-start(f32[32,24,80]{2,1,0:T(8,128)} %broadcast_in_dim.66), calls=%async_computation | async-start | bytes 786432 | tf_op jit(solution)/shard_map/all_to_all | solution.py:47
  14.4 0.4 copy.66
  14.8 0.8 copy-done.4
  15.6 1.2 copy.67
  17.0 11.9 %all-to-all-done = f32[32,24,80]{2,1,0:T(8,128)S(1)} async-done(((f32[32,24,80]{2,1,0:T(8,128)}), f32[32,24,80]{2,1,0:T(8,128)S(1)}, u32[]{:S(2)}, u32[]{:S(2)}) %all-to-all-start) | async-done | bytes 245792 | tf_op jit(solution)/shard_map/all_to_all | solution.py:47
  29.0 0.2 reshape.290
  29.5 0.4 copy-done.1
  30.1 0.5 fusion.47
  30.6 0.4 copy.70
  31.0 0.5 fusion.18
  31.5 0.4 copy.69
  32.1 0.6 convolution_bitcast_fusion
  32.8 0.3 reshape_reshape.3
  33.1 0.2 copy.71
  33.4 0.9 pad_maximum_fusion
  34.3 4.9 %all-to-all-start.1 = ((f32[32,24,96]{2,1,0:T(8,128)}), f32[32,24,96]{2,1,0:T(8,128)S(1)}, u32[]{:S(2)}, u32[]{:S(2)}) async-start(f32[32,24,96]{2,1,0:T(8,128)} %pad_maximum_fusion), calls=%async_computation.1 | async-start | bytes 786432 | tf_op jit(solution)/shard_map/all_to_all | solution.py:140
  39.6 1.1 fusion.48
  40.9 12.8 %all-to-all-done.1 = f32[32,24,96]{2,1,0:T(8,128)S(1)} async-done(((f32[32,24,96]{2,1,0:T(8,128)}), f32[32,24,96]{2,1,0:T(8,128)S(1)}, u32[]{:S(2)}, u32[]{:S(2)}) %all-to-all-start.1) | async-done | bytes 294944 | tf_op jit(solution)/shard_map/all_to_all | solution.py:140
  53.7 0.3 slice_reduce_fusion
  54.2 0.3 fusion.16
  54.5 0.4 convolution_bitcast_fusion.1
  55.0 0.3 reshape.297
  55.4 0.2 copy.106
  55.8 0.3 copy.105
  56.2 0.3 multiply_reduce_fusion
  56.5 0.6 gather_fusion
  57.1 0.6 gather_fusion.1
  57.7 0.3 fusion.15
  58.2 0.9 reshape.332
  59.2 4.7 %all-to-all-start.2 = ((bf16[32,2,576]{2,1,0:T(2,128)(2,1)}), bf16[32,2,576]{2,1,0:T(2,128)(2,1)S(1)}, u32[]{:S(2)}, u32[]{:S(2)}) async-start(bf16[32,2,576]{2,1,0:T(2,128)(2,1)} %reshape.332), calls=%async_computation.2 | async-start | bytes 163840 | tf_op jit(solution)/shard_map/all_to_all | solution.py:47
  63.9 9.2 %all-to-all-done.2 = bf16[32,2,576]{2,1,0:T(2,128)(2,1)S(1)} async-done(((bf16[32,2,576]{2,1,0:T(2,128)(2,1)}), bf16[32,2,576]{2,1,0:T(2,128)(2,1)S(1)}, u32[]{:S(2)}, u32[]{:S(2)}) %all-to-all-start.2) | async-done | bytes 73760 | tf_op jit(solution)/shard_map/all_to_all | solution.py:47
  73.1 32.6 %all_to_all.45 = bf16[16,96,256]{2,1,0:T(8,128)(2,1)S(1)} all-to-all(bf16[16,96,256]{2,1,0:T(8,128)(2,1)S(1)} %stack.8), channel_id=1, replica_groups=mesh['seq'=32,'req'=16] {'req'}, dimensions={0} | all-to-all | bytes 1572864 | tf_op jit(solution)/shard_map/all_to_all | solution.py:79
  105.8 25.6 %all_to_all.46 = bf16[16,96,256]{2,1,0:T(8,128)(2,1)S(1)} all-to-all(bf16[16,96,256]{2,1,0:T(8,128)(2,1)S(1)} %stack.9), channel_id=1, replica_groups=mesh['seq'=32,'req'=16] {'req'}, dimensions={0} | all-to-all | bytes 1572864 | tf_op jit(solution)/shard_map/all_to_all | solution.py:79
  131.5 1.0 stack.10
  132.4 3.6 %all-to-all-start.6 = ((bf16[16,96,256]{2,1,0:T(8,128)(2,1)}), bf16[16,96,256]{2,1,0:T(8,128)(2,1)S(1)}, u32[]{:S(2)}, u32[]{:S(2)}) async-start(bf16[16,96,256]{2,1,0:T(8,128)(2,1)} %stack.10), calls=%async_computation.6 | async-start | bytes 1572864 | tf_op jit(solution)/shard_map/all_to_all | solution.py:79
  136.1 0.2 reshape.333
  136.3 0.3 reshape.298
  136.6 0.4 copy-done.10
  137.2 0.4 reshape.334
  137.5 19.4 %all-to-all-done.6 = bf16[16,96,256]{2,1,0:T(8,128)(2,1)S(1)} async-done(((bf16[16,96,256]{2,1,0:T(8,128)(2,1)}), bf16[16,96,256]{2,1,0:T(8,128)(2,1)S(1)}, u32[]{:S(2)}, u32[]{:S(2)}) %all-to-all-start.6) | async-done | bytes 786464 | tf_op jit(solution)/shard_map/all_to_all | solution.py:79
  156.9 14.9 %all_to_all.47 = f32[32,1,1152]{2,1,0:T(1,128)S(1)} all-to-all(f32[32,1,1152]{2,1,0:T(1,128)S(1)} %reshape.334), channel_id=1, replica_groups=mesh['seq'=32,'req'=16] {'seq'}, dimensions={0} | all-to-all | bytes 294912 | tf_op jit(solution)/shard_map/all_to_all | solution.py:47
  171.8 1.0 stack.11
  172.8 4.6 %all-to-all-start.7 = ((bf16[16,96,256]{2,1,0:T(8,128)(2,1)}), bf16[16,96,256]{2,1,0:T(8,128)(2,1)}, u32[]{:S(2)}, u32[]{:S(2)}) async-start(bf16[16,96,256]{2,1,0:T(8,128)(2,1)} %stack.11), calls=%async_computation.7 | async-start | bytes 1572864 | tf_op jit(solution)/shard_map/all_to_all | solution.py:79
  177.6 35.1 %all-gather = bf16[1,256,1536]{1,2,0:T(8,128)(2,1)} all-gather(bf16[1,256,96]{1,2,0:T(8,128)(2,1)S(1)} %get-tuple-element.20), channel_id=2, replica_groups=mesh['seq'=32,'req'=16] {'req'}, dimensions={2}, use_global_device_ids=true | all-gather | bytes 835584 | tf_op jit(solution)/shard_map/all_gather | solution.py:87
  212.8 18.1 %all-gather.1 = bf16[1,256,1536]{1,2,0:T(8,128)(2,1)} all-gather(bf16[1,256,96]{1,2,0:T(8,128)(2,1)S(1)} %get-tuple-element.21), channel_id=3, replica_groups=mesh['seq'=32,'req'=16] {'req'}, dimensions={2}, use_global_device_ids=true | all-gather | bytes 835584 | tf_op jit(solution)/shard_map/all_gather | solution.py:87
  230.8 0.5 broadcast.251
  231.3 1.0 reduce.5
  232.3 0.2 reshape.335
  232.6 0.2 reshape.299
  232.8 0.3 reshape.300
  233.1 0.7 add.165
  234.0 3.1 %fusion = f32[24,1024]{1,0:T(8,128)S(1)} fusion(bf16[1536,256]{1,0:T(8,128)(2,1)} %bitcast.26, bf16[1536,256]{1,0:T(8,128)(2,1)S(1)} %bitcast.79, bf16[1536,256]{1,0:T(8,128)(2,1)S(1)} %bitcast.78, bf16[1536,256]{1,0:T(8,128)(2,1)S(1)} %bitcast.77, f32[24,1536]{1,0:T(8,128)} %add.165, f32[1536]{0:T(1024)S(1)} %copy-done.16, f32[24]{0:T(128)S(1)} %rsqrt.25), kind=kOutput, calls=%fused_computation.2 | convolution fusion | flops 88190976 | bytes 3397728 | tf_op jit(solution)/shard_map/dot_general | solution.py:177
  237.2 0.5 convolution_multiply_fusion
  237.7 0.2 reshape.305
  237.9 0.2 copy.120
  238.1 0.4 reshape.336
  238.5 14.8 %all_to_all.48 = f32[32,1,1152]{2,1,0:T(1,128)S(1)} all-to-all(f32[32,1,1152]{2,1,0:T(1,128)S(1)} %reshape.336), channel_id=1, replica_groups=mesh['seq'=32,'req'=16] {'seq'}, dimensions={0} | all-to-all | bytes 294912 | tf_op jit(solution)/shard_map/all_to_all | solution.py:56
  253.3 1.0 reduce.6
  254.3 0.2 reshape.337
  254.6 1.4 add_convert_fusion.2
  (95 shorter events, 4.0 us)
Async XLA Ops:
  0.0 2.0 copy-start
  2.0 12.0 %copy-start.15 = (s32[6]{0:T(128)S(1)}, s32[6]{0:T(128)}, u32[]{:S(2)}) copy-start(s32[6]{0:T(128)} %param.21) | copy-start | bytes 76
  2.0 12.1 %copy-start.14 = (s32[6,8]{1,0:T(8,128)S(1)}, s32[6,8]{1,0:T(8,128)}, u32[]{:S(2)}) copy-start(s32[6,8]{1,0:T(8,128)} %param.20) | copy-start | bytes 580
  2.1 12.4 %copy-start.3 = (bf16[6,128,512]{2,1,0:T(8,128)(2,1)S(1)}, bf16[6,128,512]{2,1,0:T(8,128)(2,1)}, u32[]{:S(2)}) copy-start(bf16[6,128,512]{2,1,0:T(8,128)(2,1)} %param.18) | copy-start | bytes 2359300
  3.9 25.1 %all-to-all-start = ((f32[32,24,80]{2,1,0:T(8,128)}), f32[32,24,80]{2,1,0:T(8,128)S(1)}, u32[]{:S(2)}, u32[]{:S(2)}) async-start(f32[32,24,80]{2,1,0:T(8,128)} %broadcast_in_dim.66), calls=%async_computation | async-start | bytes 786432 | tf_op jit(solution)/shard_map/all_to_all | solution.py:47
  14.4 1.1 copy-start.4
  29.2 0.7 copy-start.1
  30.6 1.5 copy-start.5
  33.4 5.8 %slice-start = ((f32[24,2560]{1,0:T(8,128)}), f32[24,512]{1,0:T(8,128)S(1)}, s32[]{:S(2)}) async-start(f32[24,2560]{1,0:T(8,128)} %copy-done.1), calls=%async_computation.9 | async-start | bytes 98304 | tf_op jit(solution)/shard_map/slice | solution.py:100
  34.3 5.1 %copy-start.2 = (f32[24,2560]{1,0:T(8,128)S(1)}, f32[24,2560]{1,0:T(8,128)}, u32[]{:S(2)}) copy-start(f32[24,2560]{1,0:T(8,128)} %copy-done.1) | copy-start | bytes 737284
  34.3 19.4 %all-to-all-start.1 = ((f32[32,24,96]{2,1,0:T(8,128)}), f32[32,24,96]{2,1,0:T(8,128)S(1)}, u32[]{:S(2)}, u32[]{:S(2)}) async-start(f32[32,24,96]{2,1,0:T(8,128)} %pad_maximum_fusion), calls=%async_computation.1 | async-start | bytes 786432 | tf_op jit(solution)/shard_map/all_to_all | solution.py:140
  57.7 6.1 %copy-start.9 = (bf16[1,96,1024]{2,1,0:T(8,128)(2,1)S(1)}, bf16[1,96,1024]{2,1,0:T(8,128)(2,1)}, u32[]{:S(2)}) copy-start(bf16[1,96,1024]{2,1,0:T(8,128)(2,1)} %param.24) | copy-start | bytes 589828
  59.2 13.9 %all-to-all-start.2 = ((bf16[32,2,576]{2,1,0:T(2,128)(2,1)}), bf16[32,2,576]{2,1,0:T(2,128)(2,1)S(1)}, u32[]{:S(2)}, u32[]{:S(2)}) async-start(bf16[32,2,576]{2,1,0:T(2,128)(2,1)} %reshape.332), calls=%async_computation.2 | async-start | bytes 163840 | tf_op jit(solution)/shard_map/all_to_all | solution.py:47
  132.4 24.5 %all-to-all-start.6 = ((bf16[16,96,256]{2,1,0:T(8,128)(2,1)}), bf16[16,96,256]{2,1,0:T(8,128)(2,1)S(1)}, u32[]{:S(2)}, u32[]{:S(2)}) async-start(bf16[16,96,256]{2,1,0:T(8,128)(2,1)} %stack.10), calls=%async_computation.6 | async-start | bytes 1572864 | tf_op jit(solution)/shard_map/all_to_all | solution.py:79
  136.0 0.9 copy-start.10
  172.8 4.6 %copy-start.12 = (f32[6,4,8]{2,1,0:T(4,128)S(1)}, f32[6,4,8]{2,1,0:T(4,128)}, u32[]{:S(2)}) copy-start(f32[6,4,8]{2,1,0:T(4,128)} %param.23) | copy-start | bytes 2308
  172.8 4.6 %copy-start.13 = (s32[6,4,8]{2,1,0:T(4,128)S(1)}, s32[6,4,8]{2,1,0:T(4,128)}, u32[]{:S(2)}) copy-start(s32[6,4,8]{2,1,0:T(4,128)} %param.22) | copy-start | bytes 2308
  172.8 4.8 %copy-start.11 = (bf16[1,512,96]{1,2,0:T(8,128)(2,1)S(1)}, bf16[1,512,96]{1,2,0:T(8,128)(2,1)}, u32[]{:S(2)}) copy-start(bf16[1,512,96]{1,2,0:T(8,128)(2,1)} %param.25) | copy-start | bytes 294916
  172.8 61.2 %all-to-all-start.7 = ((bf16[16,96,256]{2,1,0:T(8,128)(2,1)}), bf16[16,96,256]{2,1,0:T(8,128)(2,1)}, u32[]{:S(2)}, u32[]{:S(2)}) async-start(bf16[16,96,256]{2,1,0:T(8,128)(2,1)} %stack.11), calls=%async_computation.7 | async-start | bytes 1572864 | tf_op jit(solution)/shard_map/all_to_all | solution.py:79
  232.6 1.2 copy-start.8
  232.6 1.4 copy-start.16
  234.0 3.2 %copy-start.6 = (bf16[1,256,1536]{1,2,0:T(8,128)(2,1)S(1)}, bf16[1,256,1536]{1,2,0:T(8,128)(2,1)}, u32[]{:S(2)}) copy-start(bf16[1,256,1536]{1,2,0:T(8,128)(2,1)} %all-gather) | copy-start | bytes 2359300
  234.0 3.2 %copy-start.7 = (bf16[1,256,1536]{1,2,0:T(8,128)(2,1)S(1)}, bf16[1,256,1536]{1,2,0:T(8,128)(2,1)}, u32[]{:S(2)}) copy-start(bf16[1,256,1536]{1,2,0:T(8,128)(2,1)} %all-gather.1) | copy-start | bytes 2359300
